TPU v7x, 256 devices: a whole 4x4x8 slice. The times are simulated.
256 devices in a mesh: energy: 32 (over x, y, core), space: 8 (over z).
Axes of the slice: x: 4, y: 4, z: 8, core: 2. Of those that a mesh axis runs over, the one named last changes fastest.
Arguments:
- onsite: float32 [8, 2, 128, 128], P('space'), may hold values from -0.25 to 0.25
- hopping: float32 [8, 2, 128, 128], P('space'), may hold values from -0.25 to 0.25
- sigma_old: float32 [32, 8, 2, 128, 128], P('energy', 'space'), may hold values from -0.0390625 to 0.0390625
- screened: float32 [32, 8, 2, 3, 2, 128, 128], P('energy', 'space'), may hold values from -1 to 1
Outputs:
- green_retarded: float32 [32, 8, 3, 2, 128, 128], P('energy', 'space')
- self_energy: float32 [32, 8, 2, 3, 2, 128, 128], P('energy', 'space')
All inputs are finite; a program needn't handle non-finite values.
Results may differ from a plain program's by a relative error of at most 0.0003.
Values sent between devices are 32-bit elements; how exact they have to be, the bound alone decides.
A program may use at most 128 MiB of HBM per device.

v0:
```python
import math
import jax
import jax.numpy as jnp
from jax import lax
from jax.sharding import PartitionSpec as P

BROADEN = 0.45
THERMAL = 0.1
PRECISE = lax.Precision.HIGHEST


def passed_along(block, axis, distance):
    devices = range(lax.axis_size(axis))
    route = [(i - distance, i) for i in devices if i - distance in devices]
    return lax.ppermute(block, axis, route)


def matmul_high(first, second):
    return jnp.matmul(first, second, precision=PRECISE)


def complex_product(first, second):
    real_part = matmul_high(first[0], second[0]) - matmul_high(first[1], second[1])
    imag_part = matmul_high(first[0], second[1]) + matmul_high(first[1], second[0])
    return jnp.stack([real_part, imag_part])


def dagger(blocks):
    return jnp.stack([jnp.swapaxes(blocks[0], -1, -2), -jnp.swapaxes(blocks[1], -1, -2)])


def invert(blocks):
    size_order = blocks.shape[-1]
    normal_complex = complex_product(dagger(blocks), blocks)
    upper_normal = jnp.concatenate([normal_complex[0], -normal_complex[1]], axis=-1)
    lower_normal = jnp.concatenate([normal_complex[1], normal_complex[0]], axis=-1)
    normal = jnp.concatenate([upper_normal, lower_normal], axis=-2)
    factor = jnp.linalg.cholesky(normal)
    right_side = jnp.concatenate(
        [jnp.swapaxes(blocks[0], -1, -2), -jnp.swapaxes(blocks[1], -1, -2)], axis=-2
    )
    middle = lax.linalg.triangular_solve(factor, right_side, left_side=True, lower=True)
    solved = lax.linalg.triangular_solve(
        factor, middle, left_side=True, lower=True, transpose_a=True
    )
    return jnp.stack([solved[..., :size_order, :], solved[..., size_order:, :]])


def spectrum_forward(cosines, sines, values):
    energies_all = values.shape[0]
    real_part = values[:, :, :, 0].reshape(energies_all, -1)
    imag_part = values[:, :, :, 1].reshape(energies_all, -1)
    return (
        matmul_high(cosines, real_part) + matmul_high(sines, imag_part),
        matmul_high(cosines, imag_part) - matmul_high(sines, real_part),
    )


def paired_inverse(system_pair, outer_pair, carried, inner_pair):
    return invert(system_pair - complex_product(outer_pair, complex_product(carried, inner_pair)))


def local(onsite, hopping, sigma_old, screened):
    local_count = sigma_old.shape[0]
    size_order = sigma_old.shape[-1]
    groups = lax.axis_size("energy")
    energies_all = local_count * groups
    segments = lax.axis_size("space")
    position = lax.axis_index("space")
    is_first = position == 0
    indices = (lax.axis_index("energy") * local_count + jnp.arange(local_count)).astype(jnp.float32)
    energy = -1.5 + 3.0 * (indices + 0.5) / energies_all
    identity = jnp.eye(size_order, dtype=jnp.float32)
    hamiltonian = 0.5 * (onsite[0] + dagger(onsite[0]))
    coupling = hopping[0]
    local_sigma = jnp.moveaxis(sigma_old[:, 0], 1, 0)
    system = jnp.stack(
        [
            energy[:, None, None] * identity - hamiltonian[0] - local_sigma[0],
            BROADEN * identity - hamiltonian[1] - local_sigma[1],
        ]
    )
    magnitude = energy * energy + BROADEN * BROADEN
    contact_green = jnp.stack(
        [
            (energy / magnitude)[:, None, None] * identity,
            (-BROADEN / magnitude)[:, None, None] * identity,
        ]
    )
    next_coupling = passed_along(coupling, "space", -1)
    system_pair = jnp.stack([system, system], axis=1)
    outer_pair = jnp.stack([dagger(coupling), next_coupling], axis=1)[:, :, None]
    inner_pair = jnp.stack([coupling, dagger(next_coupling)], axis=1)[:, :, None]

    def sweep(iteration, received):
        fresh = paired_inverse(system_pair, outer_pair, received, inner_pair)
        got_left = passed_along(fresh[:, 0], "space", 1)
        got_left = jnp.where(is_first, contact_green, got_left)
        got_right = passed_along(fresh[:, 1], "space", -1)
        return jnp.stack([got_left, got_right], axis=1)

    start_left = jnp.where(is_first, contact_green, jnp.zeros_like(contact_green))
    start_pair = jnp.stack([start_left, jnp.zeros_like(contact_green)], axis=1)
    final_pair = lax.fori_loop(0, segments - 1, sweep, start_pair)
    previous = final_pair[:, 0]
    following = final_pair[:, 1]
    self_left = complex_product(dagger(coupling), complex_product(previous, coupling))
    self_right = complex_product(next_coupling, complex_product(following, dagger(next_coupling)))
    diagonal = invert(system - self_left - self_right)
    upper_block = complex_product(previous, complex_product(coupling, diagonal))
    lower_block = complex_product(diagonal, complex_product(dagger(coupling), previous))
    stacked = jnp.stack([diagonal, upper_block, lower_block], axis=2)
    green_out = jnp.transpose(stacked, (1, 2, 0, 3, 4))[:, None]
    spectral = jnp.stack(
        [
            diagonal - dagger(diagonal),
            upper_block - dagger(lower_block),
            lower_block - dagger(upper_block),
        ],
        axis=2,
    )
    kernels = screened.reshape(local_count, 2, 3, 2, size_order * size_order)
    occupation = 1.0 / (1.0 + jnp.exp(energy / THERMAL))
    occupied = occupation[None, :, None, None, None]
    both_kinds = jnp.stack([-occupied * spectral, (1.0 - occupied) * spectral])
    outgoing = jnp.transpose(both_kinds, (2, 0, 3, 1, 4, 5)).reshape(
        local_count, 2, 3, 2, size_order * size_order
    )
    gathered, spectra = (
        lax.all_to_all(outgoing, "energy", split_axis=4, concat_axis=0, tiled=True),
        lax.all_to_all(kernels, "energy", split_axis=4, concat_axis=0, tiled=True),
    )
    padded_length = 2 * energies_all
    frequency = jnp.arange(padded_length, dtype=jnp.int32)[:, None]
    position_grid = jnp.arange(energies_all, dtype=jnp.int32)[None, :]
    phases = (frequency * position_grid % padded_length).astype(jnp.float32) * (
        2.0 * math.pi / padded_length
    )
    cosines = jnp.cos(phases)
    sines = jnp.sin(phases)
    green_real, green_imag = spectrum_forward(cosines, sines, gathered)
    kernel_real, kernel_imag = spectrum_forward(cosines, sines, spectra)
    product_real = green_real * kernel_real - green_imag * kernel_imag
    product_imag = green_real * kernel_imag + green_imag * kernel_real
    back_cosines = jnp.transpose(cosines) / padded_length
    back_sines = jnp.transpose(sines) / padded_length
    conv_real = matmul_high(back_cosines, product_real) - matmul_high(back_sines, product_imag)
    conv_imag = matmul_high(back_cosines, product_imag) + matmul_high(back_sines, product_real)
    slice_width = gathered.shape[-1]
    conv_real = conv_real.reshape(energies_all, 2, 3, slice_width)
    conv_imag = conv_imag.reshape(energies_all, 2, 3, slice_width)
    sigma_elements = jnp.stack([-conv_imag, conv_real], axis=3)
    sigma_local = lax.all_to_all(sigma_elements, "energy", split_axis=0, concat_axis=4, tiled=True)
    sigma_out = sigma_local.reshape(local_count, 1, 2, 3, 2, size_order, size_order)
    return (green_out, sigma_out)


def solution(mesh):
    placed = (
        P("space", None, None, None),
        P("space", None, None, None),
        P("energy", "space", None, None, None),
        P("energy", "space", None, None, None, None, None),
    )
    return jax.shard_map(
        local,
        mesh=mesh,
        in_specs=placed,
        out_specs=(
            P("energy", "space", None, None, None, None),
            P("energy", "space", None, None, None, None, None),
        ),
        check_vma=False,
    )
```

profile of v0, /device:TPU:1, one launch (start us, length us, event | category | flops | bytes accessed | tf_op | source)
XLA Modules:
  0.0 1384.2 jit_solution(7943360227580603645)
XLA Ops:
  3.1 24.3 %copy.351 = f32[1,1,2,3,2,128,128]{3,4,2,6,5,1,0:T(2,128)} copy(f32[1,1,2,3,2,128,128]{6,5,4,3,2,1,0:T(8,128)} %param.9) | data formatting | bytes 1572864 | tf_op args[3]
  27.5 50.3 %reshape.1289 = f32[32,1,6144]{2,1,0:T(1,128)} reshape(f32[16384,1,2,2,3]{4,3,2,1,0:T(2,128)} %bitcast.664) | data formatting | bytes 1572864
  77.7 8.6 all-to-all-start.1
  87.5 894.0 %while.14 = (s32[]{:T(128)}, f32[2,2,1,128,128]{4,3,0,2,1:T(8,128)S(1)}, pred[]{:T(512)}, f32[2,2,1,128,128]{4,3,1,2,0:T(8,128)S(1)}, f32[2,2,1,128,128]{4,3,1,2...) while((s32[]{:T(128)}, ...), condition=%wide.region_5.6_spmd, body=%wide.region_0.5_spmd.sunk | while | flops 1009058304 | bytes 19206544 | solution.py:104
  92.7 23.5 %custom-call.47 = f32[2,1,128,128]{3,2,1,0:T(8,128)S(1)} custom-call(f32[2,1,128,128]{3,2,1,0:T(8,128)S(1)} %cholesky.395), custom_call_target="Cholesky" | custom-call | tf_op jit(solution)/shard_map/while/body/eval_jaxpr/jit(cholesky)/cholesky | solution.py:38
  116.3 19.7 %custom-call.48 = f32[2,1,1,128,128]{3,4,2,1,0:T(8,128)S(1)} custom-call(f32[2,1,1,128,128]{4,3,2,1,0:T(8,128)S(1)} %select_bitcast_fusion.7), custom_call_target="InvertDiagBlocksLowerTriangular" | custom-call | tf_op jit(solution)/shard_map/while/body/eval_jaxpr/jit(cholesky)/cholesky | solution.py:38
  136.6 23.5 %custom-call.49 = f32[2,1,128,128]{3,2,1,0:T(8,128)S(1)} custom-call(f32[2,1,128,128]{3,2,1,0:T(8,128)S(1)} %fusion.435), custom_call_target="Cholesky" | custom-call | tf_op jit(solution)/shard_map/while/body/eval_jaxpr/jit(cholesky)/cholesky | solution.py:38
  164.5 39.3 %custom-call.51 = f32[2,1,2,128,128]{3,4,2,1,0:T(8,128)S(1)} custom-call(f32[2,1,2,128,128]{4,3,2,1,0:T(8,128)S(1)} %bitcast.691), custom_call_target="InvertDiagBlocksLowerTriangular" | custom-call | tf_op jit(solution)/shard_map/while/body/eval_jaxpr/triangular_solve | solution.py:43
  205.9 4.3 collective-permute-start.1
  221.7 23.5 %custom-call.47 = f32[2,1,128,128]{3,2,1,0:T(8,128)S(1)} custom-call(f32[2,1,128,128]{3,2,1,0:T(8,128)S(1)} %cholesky.395), custom_call_target="Cholesky" | custom-call | tf_op jit(solution)/shard_map/while/body/eval_jaxpr/jit(cholesky)/cholesky | solution.py:38
  245.2 19.7 %custom-call.48 = f32[2,1,1,128,128]{3,4,2,1,0:T(8,128)S(1)} custom-call(f32[2,1,1,128,128]{4,3,2,1,0:T(8,128)S(1)} %select_bitcast_fusion.7), custom_call_target="InvertDiagBlocksLowerTriangular" | custom-call | tf_op jit(solution)/shard_map/while/body/eval_jaxpr/jit(cholesky)/cholesky | solution.py:38
  265.5 23.5 %custom-call.49 = f32[2,1,128,128]{3,2,1,0:T(8,128)S(1)} custom-call(f32[2,1,128,128]{3,2,1,0:T(8,128)S(1)} %fusion.435), custom_call_target="Cholesky" | custom-call | tf_op jit(solution)/shard_map/while/body/eval_jaxpr/jit(cholesky)/cholesky | solution.py:38
  293.4 39.3 %custom-call.51 = f32[2,1,2,128,128]{3,4,2,1,0:T(8,128)S(1)} custom-call(f32[2,1,2,128,128]{4,3,2,1,0:T(8,128)S(1)} %bitcast.691), custom_call_target="InvertDiagBlocksLowerTriangular" | custom-call | tf_op jit(solution)/shard_map/while/body/eval_jaxpr/triangular_solve | solution.py:43
  340.3 5.3 collective-permute-done
  350.4 23.5 %custom-call.47 = f32[2,1,128,128]{3,2,1,0:T(8,128)S(1)} custom-call(f32[2,1,128,128]{3,2,1,0:T(8,128)S(1)} %cholesky.395), custom_call_target="Cholesky" | custom-call | tf_op jit(solution)/shard_map/while/body/eval_jaxpr/jit(cholesky)/cholesky | solution.py:38
  373.9 19.7 %custom-call.48 = f32[2,1,1,128,128]{3,4,2,1,0:T(8,128)S(1)} custom-call(f32[2,1,1,128,128]{4,3,2,1,0:T(8,128)S(1)} %select_bitcast_fusion.7), custom_call_target="InvertDiagBlocksLowerTriangular" | custom-call | tf_op jit(solution)/shard_map/while/body/eval_jaxpr/jit(cholesky)/cholesky | solution.py:38
  394.2 23.5 %custom-call.49 = f32[2,1,128,128]{3,2,1,0:T(8,128)S(1)} custom-call(f32[2,1,128,128]{3,2,1,0:T(8,128)S(1)} %fusion.435), custom_call_target="Cholesky" | custom-call | tf_op jit(solution)/shard_map/while/body/eval_jaxpr/jit(cholesky)/cholesky | solution.py:38
  422.1 39.3 %custom-call.51 = f32[2,1,2,128,128]{3,4,2,1,0:T(8,128)S(1)} custom-call(f32[2,1,2,128,128]{4,3,2,1,0:T(8,128)S(1)} %bitcast.691), custom_call_target="InvertDiagBlocksLowerTriangular" | custom-call | tf_op jit(solution)/shard_map/while/body/eval_jaxpr/triangular_solve | solution.py:43
  463.5 4.3 collective-permute-start.1
  478.3 23.5 %custom-call.47 = f32[2,1,128,128]{3,2,1,0:T(8,128)S(1)} custom-call(f32[2,1,128,128]{3,2,1,0:T(8,128)S(1)} %cholesky.395), custom_call_target="Cholesky" | custom-call | tf_op jit(solution)/shard_map/while/body/eval_jaxpr/jit(cholesky)/cholesky | solution.py:38
  501.8 19.7 %custom-call.48 = f32[2,1,1,128,128]{3,4,2,1,0:T(8,128)S(1)} custom-call(f32[2,1,1,128,128]{4,3,2,1,0:T(8,128)S(1)} %select_bitcast_fusion.7), custom_call_target="InvertDiagBlocksLowerTriangular" | custom-call | tf_op jit(solution)/shard_map/while/body/eval_jaxpr/jit(cholesky)/cholesky | solution.py:38
  522.2 23.5 %custom-call.49 = f32[2,1,128,128]{3,2,1,0:T(8,128)S(1)} custom-call(f32[2,1,128,128]{3,2,1,0:T(8,128)S(1)} %fusion.435), custom_call_target="Cholesky" | custom-call | tf_op jit(solution)/shard_map/while/body/eval_jaxpr/jit(cholesky)/cholesky | solution.py:38
  550.1 39.3 %custom-call.51 = f32[2,1,2,128,128]{3,4,2,1,0:T(8,128)S(1)} custom-call(f32[2,1,2,128,128]{4,3,2,1,0:T(8,128)S(1)} %bitcast.691), custom_call_target="InvertDiagBlocksLowerTriangular" | custom-call | tf_op jit(solution)/shard_map/while/body/eval_jaxpr/triangular_solve | solution.py:43
  605.6 23.5 %custom-call.47 = f32[2,1,128,128]{3,2,1,0:T(8,128)S(1)} custom-call(f32[2,1,128,128]{3,2,1,0:T(8,128)S(1)} %cholesky.395), custom_call_target="Cholesky" | custom-call | tf_op jit(solution)/shard_map/while/body/eval_jaxpr/jit(cholesky)/cholesky | solution.py:38
  629.1 19.7 %custom-call.48 = f32[2,1,1,128,128]{3,4,2,1,0:T(8,128)S(1)} custom-call(f32[2,1,1,128,128]{4,3,2,1,0:T(8,128)S(1)} %select_bitcast_fusion.7), custom_call_target="InvertDiagBlocksLowerTriangular" | custom-call | tf_op jit(solution)/shard_map/while/body/eval_jaxpr/jit(cholesky)/cholesky | solution.py:38
  649.4 23.5 %custom-call.49 = f32[2,1,128,128]{3,2,1,0:T(8,128)S(1)} custom-call(f32[2,1,128,128]{3,2,1,0:T(8,128)S(1)} %fusion.435), custom_call_target="Cholesky" | custom-call | tf_op jit(solution)/shard_map/while/body/eval_jaxpr/jit(cholesky)/cholesky | solution.py:38
  677.3 39.3 %custom-call.51 = f32[2,1,2,128,128]{3,4,2,1,0:T(8,128)S(1)} custom-call(f32[2,1,2,128,128]{4,3,2,1,0:T(8,128)S(1)} %bitcast.691), custom_call_target="InvertDiagBlocksLowerTriangular" | custom-call | tf_op jit(solution)/shard_map/while/body/eval_jaxpr/triangular_solve | solution.py:43
  732.9 23.5 %custom-call.47 = f32[2,1,128,128]{3,2,1,0:T(8,128)S(1)} custom-call(f32[2,1,128,128]{3,2,1,0:T(8,128)S(1)} %cholesky.395), custom_call_target="Cholesky" | custom-call | tf_op jit(solution)/shard_map/while/body/eval_jaxpr/jit(cholesky)/cholesky | solution.py:38
  756.4 19.7 %custom-call.48 = f32[2,1,1,128,128]{3,4,2,1,0:T(8,128)S(1)} custom-call(f32[2,1,1,128,128]{4,3,2,1,0:T(8,128)S(1)} %select_bitcast_fusion.7), custom_call_target="InvertDiagBlocksLowerTriangular" | custom-call | tf_op jit(solution)/shard_map/while/body/eval_jaxpr/jit(cholesky)/cholesky | solution.py:38
  776.8 23.5 %custom-call.49 = f32[2,1,128,128]{3,2,1,0:T(8,128)S(1)} custom-call(f32[2,1,128,128]{3,2,1,0:T(8,128)S(1)} %fusion.435), custom_call_target="Cholesky" | custom-call | tf_op jit(solution)/shard_map/while/body/eval_jaxpr/jit(cholesky)/cholesky | solution.py:38
  804.6 39.3 %custom-call.51 = f32[2,1,2,128,128]{3,4,2,1,0:T(8,128)S(1)} custom-call(f32[2,1,2,128,128]{4,3,2,1,0:T(8,128)S(1)} %bitcast.691), custom_call_target="InvertDiagBlocksLowerTriangular" | custom-call | tf_op jit(solution)/shard_map/while/body/eval_jaxpr/triangular_solve | solution.py:43
  859.3 23.5 %custom-call.47 = f32[2,1,128,128]{3,2,1,0:T(8,128)S(1)} custom-call(f32[2,1,128,128]{3,2,1,0:T(8,128)S(1)} %cholesky.395), custom_call_target="Cholesky" | custom-call | tf_op jit(solution)/shard_map/while/body/eval_jaxpr/jit(cholesky)/cholesky | solution.py:38
  882.8 19.7 %custom-call.48 = f32[2,1,1,128,128]{3,4,2,1,0:T(8,128)S(1)} custom-call(f32[2,1,1,128,128]{4,3,2,1,0:T(8,128)S(1)} %select_bitcast_fusion.7), custom_call_target="InvertDiagBlocksLowerTriangular" | custom-call | tf_op jit(solution)/shard_map/while/body/eval_jaxpr/jit(cholesky)/cholesky | solution.py:38
  903.2 23.5 %custom-call.49 = f32[2,1,128,128]{3,2,1,0:T(8,128)S(1)} custom-call(f32[2,1,128,128]{3,2,1,0:T(8,128)S(1)} %fusion.435), custom_call_target="Cholesky" | custom-call | tf_op jit(solution)/shard_map/while/body/eval_jaxpr/jit(cholesky)/cholesky | solution.py:38
  931.1 39.3 %custom-call.51 = f32[2,1,2,128,128]{3,4,2,1,0:T(8,128)S(1)} custom-call(f32[2,1,2,128,128]{4,3,2,1,0:T(8,128)S(1)} %bitcast.691), custom_call_target="InvertDiagBlocksLowerTriangular" | custom-call | tf_op jit(solution)/shard_map/while/body/eval_jaxpr/triangular_solve | solution.py:43
  987.0 11.7 custom-call.36
  999.3 9.8 custom-call.37
  1009.6 11.9 custom-call.38
  1028.0 19.7 %custom-call.39 = f32[1,2,128,128]{2,3,1,0:T(8,128)S(1)} custom-call(f32[1,2,128,128]{3,2,1,0:T(8,128)S(1)} %bitcast.692), custom_call_target="InvertDiagBlocksLowerTriangular" | custom-call | tf_op jit(solution)/shard_map/triangular_solve | solution.py:43
  1055.1 30.3 %copy.347 = f32[1,2,3,2,16384]{2,3,1,0,4:T(2,128)} copy(f32[1,2,3,2,16384]{4,0,3,2,1:T(1,128)S(1)} %bitcast.676) | data formatting | bytes 1572864 | tf_op jit(solution)/shard_map/reshape | solution.py:126
  1085.4 50.3 %reshape.1287 = f32[32,1,6144]{2,1,0:T(1,128)} reshape(f32[16384,1,2,2,3]{4,3,2,1,0:T(2,128)} %bitcast.661) | data formatting | bytes 1572864
  1135.7 17.0 %all-to-all-start = ((f32[32,1,6144]{2,1,0:T(1,128)}), f32[32,1,6144]{2,1,0:T(1,128)S(1)}, u32[]{:S(2)}, u32[]{:S(2)}) async-start(f32[32,1,6144]{2,1,0:T(1,128)} %reshape.1287), calls=%async_computation | async-start | bytes 1572864 | tf_op jit(solution)/shard_map/all_to_all | solution.py:130
  1156.8 64.8 %reshape.1290 = f32[16384,1,2,2,3]{4,3,2,1,0:T(2,128)} reshape(f32[32,6144]{1,0:T(8,128)S(1)} %reduce.36) | data formatting | bytes 1572864
  1221.6 26.7 %copy.380 = f32[1,2,3,2,32,512]{5,4,3,2,1,0:T(8,128)S(1)} copy(f32[1,2,3,2,32,512]{2,3,1,5,4,0:T(2,128)} %bitcast.662) | data formatting | bytes 1572864 | tf_op jit(solution)/shard_map/all_to_all | solution.py:131
  1255.7 65.0 %reshape.1288 = f32[16384,1,2,2,3]{4,3,2,1,0:T(2,128)} reshape(f32[32,6144]{1,0:T(8,128)S(1)} %reduce.37) | data formatting | bytes 1572864
  1320.7 26.9 %copy.379 = f32[1,2,3,2,32,512]{5,4,3,2,1,0:T(8,128)S(1)} copy(f32[1,2,3,2,32,512]{2,3,1,5,4,0:T(2,128)} %bitcast.663) | data formatting | bytes 1572864 | tf_op jit(solution)/shard_map/all_to_all | solution.py:130
  1361.1 7.4 all-to-all-start.2
  1369.7 13.1 all-to-all-done.2
  (527 shorter events, 216.4 us)
Async XLA Ops:
  1.6 84.8 %copy-start = (f32[1,2,128,128]{3,2,1,0:T(8,128)S(1)}, f32[1,2,128,128]{3,2,1,0:T(8,128)}, u32[]{:S(2)}) copy-start(f32[1,2,128,128]{3,2,1,0:T(8,128)} %param.7) | copy-start | bytes 393220
  1.6 84.9 %copy-start.9 = (f32[1,2,128,128]{3,2,1,0:T(8,128)S(1)}, f32[1,2,128,128]{3,2,1,0:T(8,128)}, u32[]{:S(2)}) copy-start(f32[1,2,128,128]{3,2,1,0:T(8,128)} %param.6) | copy-start | bytes 393220
  1.7 85.2 %copy-start.11 = (f32[1,1,2,128,128]{4,3,2,1,0:T(8,128)S(1)}, f32[1,1,2,128,128]{4,3,2,1,0:T(8,128)}, u32[]{:S(2)}) copy-start(f32[1,1,2,128,128]{4,3,2,1,0:T(8,128)} %param.8) | copy-start | bytes 393220
  1.7 85.6 %collective-permute-start.2 = (f32[2,128,128]{1,2,0:T(8,128)S(1)}, f32[2,128,128]{1,2,0:T(8,128)S(1)}, u32[]{:S(2)}, u32[]{:S(2)}) collective-permute-start(f32[2,128,128]{1,2,0:T(8,128)S(1)} %bitcast.690), channel_id=1, source_target_pairs={{1,0},{2,1},{3,2},{4,3},{5,4},{6,5},{7,6},{9,8},{10,9},{11,10},{12... | collective-permute-start | bytes 393224 | tf_op jit(solution)/shard_map/ppermute | solution.py:15
  77.7 1057.9 %all-to-all-start.1 = ((f32[32,1,6144]{2,1,0:T(1,128)}), f32[32,1,6144]{2,1,0:T(1,128)}, u32[]{:S(2)}, u32[]{:S(2)}) async-start(f32[32,1,6144]{2,1,0:T(1,128)} %reshape.1289), calls=%async_computation.1 | async-start | bytes 1572864 | tf_op jit(solution)/shard_map/all_to_all | solution.py:131
  205.9 6.8 collective-permute-start.1
  210.1 6.7 collective-permute-start
  334.8 5.5 collective-permute-start.1
  338.4 7.2 collective-permute-start
  463.5 6.2 collective-permute-start.1
  467.8 5.7 collective-permute-start
  591.4 5.5 collective-permute-start.1
  595.0 5.8 collective-permute-start
  718.7 5.6 collective-permute-start.1
  722.4 5.7 collective-permute-start
  846.0 4.7 collective-permute-start.1
  848.8 5.7 collective-permute-start
  972.4 5.1 collective-permute-start.1
  975.6 5.7 collective-permute-start
  1051.3 3.1 copy-start.1
  1051.5 2.8 copy-start.3
  1054.0 0.6 copy-start.5
  1054.1 0.6 copy-start.7
  1135.7 117.5 %all-to-all-start = ((f32[32,1,6144]{2,1,0:T(1,128)}), f32[32,1,6144]{2,1,0:T(1,128)S(1)}, u32[]{:S(2)}, u32[]{:S(2)}) async-start(f32[32,1,6144]{2,1,0:T(1,128)} %reshape.1287), calls=%async_computation | async-start | bytes 1572864 | tf_op jit(solution)/shard_map/all_to_all | solution.py:130
  1320.7 47.8 %copy-start.10 = (f32[2,1,1,128,128]{4,3,0,2,1:T(8,128)S(1)}, f32[2,1,1,128,128]{4,3,0,2,1:T(8,128)}, u32[]{:S(2)}) copy-start(f32[2,1,1,128,128]{4,3,0,2,1:T(8,128)} %get-tuple-element.173) | copy-start | bytes 393220
  1320.7 47.9 %copy-start.2 = (f32[128,128]{0,1:T(8,128)S(1)}, f32[128,128]{0,1:T(8,128)}, u32[]{:S(2)}) copy-start(f32[128,128]{0,1:T(8,128)} %copy-done.1) | copy-start | bytes 196612
  1320.7 47.9 %copy-start.4 = (f32[128,128]{0,1:T(8,128)S(1)}, f32[128,128]{0,1:T(8,128)}, u32[]{:S(2)}) copy-start(f32[128,128]{0,1:T(8,128)} %copy-done.3) | copy-start | bytes 196612
  1320.7 48.0 %copy-start.6 = (f32[128,128]{0,1:T(8,128)S(1)}, f32[128,128]{0,1:T(8,128)}, u32[]{:S(2)}) copy-start(f32[128,128]{0,1:T(8,128)} %copy-done.5) | copy-start | bytes 196612
  1320.7 48.0 %copy-start.8 = (f32[1,1,128,128]{2,3,0,1:T(8,128)S(1)}, f32[1,1,128,128]{2,3,0,1:T(8,128)}, u32[]{:S(2)}) copy-start(f32[1,1,128,128]{2,3,0,1:T(8,128)} %copy-done.7) | copy-start | bytes 196612
  1361.1 21.6 %all-to-all-start.2 = ((f32[32,2,3,2,512]{4,3,2,1,0:T(2,128)}), f32[32,2,3,2,512]{4,3,2,1,0:T(2,128)S(1)}, u32[]{:S(2)}, u32[]{:S(2)}) async-start(f32[32,2,3,2,512]{4,3,2,1,0:T(2,128)} %copy.355), calls=%async_computation.2 | async-start | bytes 1572864 | tf_op jit(solution)/shard_map/all_to_all | solution.py:153
where the time goes:
time: 1390 us; the launch traced here: 1380 us
  other arithmetic  808 us (58%)
  local copies, waits for them, and re-layouts  384 us (28%)
  matrix products  70.8 us (5%)
  starting transfers between devices  68.7 us (5%)
  waiting for transfers between devices  46.4 us (3%)
    another operation x70, other arithmetic, invert(): factor = jnp.linalg.cholesky(normal)  503 us
    another operation x31, other arithmetic, invert(): lax.linalg.triangular_solve(factor, middle, left_side=True, lower=True, t...  296 us
    unnamed x33, local copies, waits for them, and re-layouts  257 us
    dot_general x132, matrix products, matmul_high(): return jnp.matmul(first, second, precision=PRECISE)  50.5 us
    ppermute x15, starting transfers between devices, passed_along(): return lax.ppermute(block, axis, route)  35.7 us
    ppermute x15, waiting for transfers between devices, passed_along(): return lax.ppermute(block, axis, route)  33.3 us
    another operation x48, local copies, waits for them, and re-layouts  31.5 us
    reshape x1, local copies, waits for them, and re-layouts, local(): jnp.transpose(both_kinds, (2, 0, 3, 1, 4, 5))  30.3 us
  transfers between devices with their start and end apart: 18, of which 15 were waited for; matrix products, arithmetic and copies ran while one was open for 83% of the time, Pallas kernels for 0%

commit v1 on v0

--- a/solution.py
+++ b/solution.py
@@ -127,7 +127,12 @@
         local_count, 2, 3, 2, size_order * size_order
     )
     gathered, spectra = (
-        lax.all_to_all(outgoing, "energy", split_axis=4, concat_axis=0, tiled=True),
+        jnp.concatenate(
+            lax.all_to_all(
+                jnp.stack(jnp.split(outgoing, lax.axis_size("energy"), axis=4)), "energy", 0, 0
+            ),
+            axis=0,
+        ),
         lax.all_to_all(kernels, "energy", split_axis=4, concat_axis=0, tiled=True),
     )
     padded_length = 2 * energies_all

time: 1390 us -> 1220 us (0.88)
  local copies, waits for them, and re-layouts: 384 us -> 218 us
    unnamed x33 -> x21, local copies, waits for them, and re-layouts: 257 us -> 142 us
    reshape x1 -> x0, local copies, waits for them, and re-layouts: 30.3 us -> none  [local(): jnp.transpose(both_kinds, (2, 0, 3, 1, 4, 5))]
    all_to_all x1 -> x0, local copies, waits for them, and re-layouts: 26.9 us -> none  [local(): lax.all_to_all(outgoing, 'energy', split_axis=4, concat_axis=0, tiled=True)]
    another operation x48 -> x52, local copies, waits for them, and re-layouts: 31.5 us -> 35.9 us
  transfers between devices with their start and end apart: 18 -> 18, of which waited for: 15 -> 15; matrix products, arithmetic and copies ran while one was open for 83% -> 89% of each run, Pallas kernels for 0% -> 0%
where the time goes in v1:
time: 1220 us
  other arithmetic  807 us (66%)
  local copies, waits for them, and re-layouts  218 us (18%)
  matrix products  71.1 us (6%)
  starting transfers between devices  68.4 us (6%)
  waiting for transfers between devices  43.8 us (4%)
    another operation x70, other arithmetic, invert(): factor = jnp.linalg.cholesky(normal)  503 us
    another operation x31, other arithmetic, invert(): lax.linalg.triangular_solve(factor, middle, left_side=True, lower=True, t...  296 us
    unnamed x21, local copies, waits for them, and re-layouts  142 us
    dot_general x132, matrix products, matmul_high(): return jnp.matmul(first, second, precision=PRECISE)  50.8 us
    ppermute x15, starting transfers between devices, passed_along(): return lax.ppermute(block, axis, route)  35.7 us
    ppermute x15, waiting for transfers between devices, passed_along(): return lax.ppermute(block, axis, route)  33.3 us
    another operation x48, local copies, waits for them, and re-layouts  32.6 us
    all_to_all x2, local copies, waits for them, and re-layouts, local(): lax.all_to_all(kernels, 'energy', split_axis=4, concat_axis=0, tiled=True)  27.3 us
  transfers between devices with their start and end apart: 18, of which 15 were waited for; matrix products, arithmetic and copies ran while one was open for 89% of the time, Pallas kernels for 0%

profile of v1, /device:TPU:1, one launch (start us, length us, event | category | flops | bytes accessed | tf_op | source)
XLA Modules:
  0.0 1215.5 jit_solution(7406681483031686523)
XLA Ops:
  3.1 24.3 %copy.289 = f32[1,1,2,3,2,128,128]{3,4,2,6,5,1,0:T(2,128)} copy(f32[1,1,2,3,2,128,128]{6,5,4,3,2,1,0:T(8,128)} %param.9) | data formatting | bytes 1572864 | tf_op args[3]
  27.4 50.3 %reshape.1293 = f32[32,1,6144]{2,1,0:T(1,128)} reshape(f32[16384,1,2,2,3]{4,3,2,1,0:T(2,128)} %bitcast.717) | data formatting | bytes 1572864
  77.7 8.6 all-to-all-start.1
  87.5 894.8 %while.14 = (s32[]{:T(128)}, f32[2,2,1,128,128]{4,3,0,2,1:T(8,128)S(1)}, pred[]{:T(512)}, f32[2,2,1,128,128]{4,3,1,2,0:T(8,128)S(1)}, f32[2,2,1,128,128]{4,3,1,2...) while((s32[]{:T(128)}, ...), condition=%wide.region_5.6_spmd, body=%wide.region_0.5_spmd.sunk | while | flops 1009058304 | bytes 19206544 | solution.py:104
  92.5 23.5 %custom-call.47 = f32[2,1,128,128]{3,2,1,0:T(8,128)S(1)} custom-call(f32[2,1,128,128]{3,2,1,0:T(8,128)S(1)} %cholesky.395), custom_call_target="Cholesky" | custom-call | tf_op jit(solution)/shard_map/while/body/eval_jaxpr/jit(cholesky)/cholesky | solution.py:38
  116.0 19.7 %custom-call.48 = f32[2,1,1,128,128]{3,4,2,1,0:T(8,128)S(1)} custom-call(f32[2,1,1,128,128]{4,3,2,1,0:T(8,128)S(1)} %select_bitcast_fusion.7), custom_call_target="InvertDiagBlocksLowerTriangular" | custom-call | tf_op jit(solution)/shard_map/while/body/eval_jaxpr/jit(cholesky)/cholesky | solution.py:38
  136.3 23.5 %custom-call.49 = f32[2,1,128,128]{3,2,1,0:T(8,128)S(1)} custom-call(f32[2,1,128,128]{3,2,1,0:T(8,128)S(1)} %fusion.434), custom_call_target="Cholesky" | custom-call | tf_op jit(solution)/shard_map/while/body/eval_jaxpr/jit(cholesky)/cholesky | solution.py:38
  164.3 39.3 %custom-call.51 = f32[2,1,2,128,128]{3,4,2,1,0:T(8,128)S(1)} custom-call(f32[2,1,2,128,128]{4,3,2,1,0:T(8,128)S(1)} %bitcast.745), custom_call_target="InvertDiagBlocksLowerTriangular" | custom-call | tf_op jit(solution)/shard_map/while/body/eval_jaxpr/triangular_solve | solution.py:43
  205.7 4.3 collective-permute-start.1
  212.5 4.2 collective-permute-done
  221.5 23.5 %custom-call.47 = f32[2,1,128,128]{3,2,1,0:T(8,128)S(1)} custom-call(f32[2,1,128,128]{3,2,1,0:T(8,128)S(1)} %cholesky.395), custom_call_target="Cholesky" | custom-call | tf_op jit(solution)/shard_map/while/body/eval_jaxpr/jit(cholesky)/cholesky | solution.py:38
  245.0 19.7 %custom-call.48 = f32[2,1,1,128,128]{3,4,2,1,0:T(8,128)S(1)} custom-call(f32[2,1,1,128,128]{4,3,2,1,0:T(8,128)S(1)} %select_bitcast_fusion.7), custom_call_target="InvertDiagBlocksLowerTriangular" | custom-call | tf_op jit(solution)/shard_map/while/body/eval_jaxpr/jit(cholesky)/cholesky | solution.py:38
  265.4 23.5 %custom-call.49 = f32[2,1,128,128]{3,2,1,0:T(8,128)S(1)} custom-call(f32[2,1,128,128]{3,2,1,0:T(8,128)S(1)} %fusion.434), custom_call_target="Cholesky" | custom-call | tf_op jit(solution)/shard_map/while/body/eval_jaxpr/jit(cholesky)/cholesky | solution.py:38
  293.4 39.3 %custom-call.51 = f32[2,1,2,128,128]{3,4,2,1,0:T(8,128)S(1)} custom-call(f32[2,1,2,128,128]{4,3,2,1,0:T(8,128)S(1)} %bitcast.745), custom_call_target="InvertDiagBlocksLowerTriangular" | custom-call | tf_op jit(solution)/shard_map/while/body/eval_jaxpr/triangular_solve | solution.py:43
  340.2 5.3 collective-permute-done
  350.3 23.5 %custom-call.47 = f32[2,1,128,128]{3,2,1,0:T(8,128)S(1)} custom-call(f32[2,1,128,128]{3,2,1,0:T(8,128)S(1)} %cholesky.395), custom_call_target="Cholesky" | custom-call | tf_op jit(solution)/shard_map/while/body/eval_jaxpr/jit(cholesky)/cholesky | solution.py:38
  373.8 19.7 %custom-call.48 = f32[2,1,1,128,128]{3,4,2,1,0:T(8,128)S(1)} custom-call(f32[2,1,1,128,128]{4,3,2,1,0:T(8,128)S(1)} %select_bitcast_fusion.7), custom_call_target="InvertDiagBlocksLowerTriangular" | custom-call | tf_op jit(solution)/shard_map/while/body/eval_jaxpr/jit(cholesky)/cholesky | solution.py:38
  394.2 23.5 %custom-call.49 = f32[2,1,128,128]{3,2,1,0:T(8,128)S(1)} custom-call(f32[2,1,128,128]{3,2,1,0:T(8,128)S(1)} %fusion.434), custom_call_target="Cholesky" | custom-call | tf_op jit(solution)/shard_map/while/body/eval_jaxpr/jit(cholesky)/cholesky | solution.py:38
  418.1 4.1 while.16
  422.2 39.3 %custom-call.51 = f32[2,1,2,128,128]{3,4,2,1,0:T(8,128)S(1)} custom-call(f32[2,1,2,128,128]{4,3,2,1,0:T(8,128)S(1)} %bitcast.745), custom_call_target="InvertDiagBlocksLowerTriangular" | custom-call | tf_op jit(solution)/shard_map/while/body/eval_jaxpr/triangular_solve | solution.py:43
  463.6 4.3 collective-permute-start.1
  478.4 23.5 %custom-call.47 = f32[2,1,128,128]{3,2,1,0:T(8,128)S(1)} custom-call(f32[2,1,128,128]{3,2,1,0:T(8,128)S(1)} %cholesky.395), custom_call_target="Cholesky" | custom-call | tf_op jit(solution)/shard_map/while/body/eval_jaxpr/jit(cholesky)/cholesky | solution.py:38
  501.9 19.7 %custom-call.48 = f32[2,1,1,128,128]{3,4,2,1,0:T(8,128)S(1)} custom-call(f32[2,1,1,128,128]{4,3,2,1,0:T(8,128)S(1)} %select_bitcast_fusion.7), custom_call_target="InvertDiagBlocksLowerTriangular" | custom-call | tf_op jit(solution)/shard_map/while/body/eval_jaxpr/jit(cholesky)/cholesky | solution.py:38
  522.2 23.5 %custom-call.49 = f32[2,1,128,128]{3,2,1,0:T(8,128)S(1)} custom-call(f32[2,1,128,128]{3,2,1,0:T(8,128)S(1)} %fusion.434), custom_call_target="Cholesky" | custom-call | tf_op jit(solution)/shard_map/while/body/eval_jaxpr/jit(cholesky)/cholesky | solution.py:38
  550.2 39.3 %custom-call.51 = f32[2,1,2,128,128]{3,4,2,1,0:T(8,128)S(1)} custom-call(f32[2,1,2,128,128]{4,3,2,1,0:T(8,128)S(1)} %bitcast.745), custom_call_target="InvertDiagBlocksLowerTriangular" | custom-call | tf_op jit(solution)/shard_map/while/body/eval_jaxpr/triangular_solve | solution.py:43
  605.7 23.5 %custom-call.47 = f32[2,1,128,128]{3,2,1,0:T(8,128)S(1)} custom-call(f32[2,1,128,128]{3,2,1,0:T(8,128)S(1)} %cholesky.395), custom_call_target="Cholesky" | custom-call | tf_op jit(solution)/shard_map/while/body/eval_jaxpr/jit(cholesky)/cholesky | solution.py:38
  629.3 19.7 %custom-call.48 = f32[2,1,1,128,128]{3,4,2,1,0:T(8,128)S(1)} custom-call(f32[2,1,1,128,128]{4,3,2,1,0:T(8,128)S(1)} %select_bitcast_fusion.7), custom_call_target="InvertDiagBlocksLowerTriangular" | custom-call | tf_op jit(solution)/shard_map/while/body/eval_jaxpr/jit(cholesky)/cholesky | solution.py:38
  649.6 23.5 %custom-call.49 = f32[2,1,128,128]{3,2,1,0:T(8,128)S(1)} custom-call(f32[2,1,128,128]{3,2,1,0:T(8,128)S(1)} %fusion.434), custom_call_target="Cholesky" | custom-call | tf_op jit(solution)/shard_map/while/body/eval_jaxpr/jit(cholesky)/cholesky | solution.py:38
  673.5 4.1 while.16
  677.6 39.3 %custom-call.51 = f32[2,1,2,128,128]{3,4,2,1,0:T(8,128)S(1)} custom-call(f32[2,1,2,128,128]{4,3,2,1,0:T(8,128)S(1)} %bitcast.745), custom_call_target="InvertDiagBlocksLowerTriangular" | custom-call | tf_op jit(solution)/shard_map/while/body/eval_jaxpr/triangular_solve | solution.py:43
  733.2 23.5 %custom-call.47 = f32[2,1,128,128]{3,2,1,0:T(8,128)S(1)} custom-call(f32[2,1,128,128]{3,2,1,0:T(8,128)S(1)} %cholesky.395), custom_call_target="Cholesky" | custom-call | tf_op jit(solution)/shard_map/while/body/eval_jaxpr/jit(cholesky)/cholesky | solution.py:38
  756.7 19.7 %custom-call.48 = f32[2,1,1,128,128]{3,4,2,1,0:T(8,128)S(1)} custom-call(f32[2,1,1,128,128]{4,3,2,1,0:T(8,128)S(1)} %select_bitcast_fusion.7), custom_call_target="InvertDiagBlocksLowerTriangular" | custom-call | tf_op jit(solution)/shard_map/while/body/eval_jaxpr/jit(cholesky)/cholesky | solution.py:38
  777.0 23.5 %custom-call.49 = f32[2,1,128,128]{3,2,1,0:T(8,128)S(1)} custom-call(f32[2,1,128,128]{3,2,1,0:T(8,128)S(1)} %fusion.434), custom_call_target="Cholesky" | custom-call | tf_op jit(solution)/shard_map/while/body/eval_jaxpr/jit(cholesky)/cholesky | solution.py:38
  805.0 39.3 %custom-call.51 = f32[2,1,2,128,128]{3,4,2,1,0:T(8,128)S(1)} custom-call(f32[2,1,2,128,128]{4,3,2,1,0:T(8,128)S(1)} %bitcast.745), custom_call_target="InvertDiagBlocksLowerTriangular" | custom-call | tf_op jit(solution)/shard_map/while/body/eval_jaxpr/triangular_solve | solution.py:43
  859.7 23.5 %custom-call.47 = f32[2,1,128,128]{3,2,1,0:T(8,128)S(1)} custom-call(f32[2,1,128,128]{3,2,1,0:T(8,128)S(1)} %cholesky.395), custom_call_target="Cholesky" | custom-call | tf_op jit(solution)/shard_map/while/body/eval_jaxpr/jit(cholesky)/cholesky | solution.py:38
  883.2 19.7 %custom-call.48 = f32[2,1,1,128,128]{3,4,2,1,0:T(8,128)S(1)} custom-call(f32[2,1,1,128,128]{4,3,2,1,0:T(8,128)S(1)} %select_bitcast_fusion.7), custom_call_target="InvertDiagBlocksLowerTriangular" | custom-call | tf_op jit(solution)/shard_map/while/body/eval_jaxpr/jit(cholesky)/cholesky | solution.py:38
  903.6 23.5 %custom-call.49 = f32[2,1,128,128]{3,2,1,0:T(8,128)S(1)} custom-call(f32[2,1,128,128]{3,2,1,0:T(8,128)S(1)} %fusion.434), custom_call_target="Cholesky" | custom-call | tf_op jit(solution)/shard_map/while/body/eval_jaxpr/jit(cholesky)/cholesky | solution.py:38
  927.5 4.1 while.16
  931.6 39.3 %custom-call.51 = f32[2,1,2,128,128]{3,4,2,1,0:T(8,128)S(1)} custom-call(f32[2,1,2,128,128]{4,3,2,1,0:T(8,128)S(1)} %bitcast.745), custom_call_target="InvertDiagBlocksLowerTriangular" | custom-call | tf_op jit(solution)/shard_map/while/body/eval_jaxpr/triangular_solve | solution.py:43
  987.8 11.7 custom-call.36
  1000.1 9.8 custom-call.37
  1010.4 11.9 custom-call.38
  1029.3 19.7 %custom-call.39 = f32[1,2,128,128]{2,3,1,0:T(8,128)S(1)} custom-call(f32[1,2,128,128]{3,2,1,0:T(8,128)S(1)} %bitcast.746), custom_call_target="InvertDiagBlocksLowerTriangular" | custom-call | tf_op jit(solution)/shard_map/triangular_solve | solution.py:43
  1059.3 16.8 %all-to-all-start = ((f32[32,1,2,3,2,512]{5,4,3,2,1,0:T(2,128)}), f32[32,1,2,3,2,512]{5,4,3,2,1,0:T(2,128)S(1)}, u32[]{:S(2)}, u32[]{:S(2)}) async-start(f32[32,1,2,3,2,512]{5,4,3,2,1,0:T(2,128)} %copy.288), calls=%async_computation | async-start | bytes 1572864 | tf_op jit(solution)/shard_map/all_to_all | solution.py:131
  1080.3 64.8 %reshape.1294 = f32[16384,1,2,2,3]{4,3,2,1,0:T(2,128)} reshape(f32[32,6144]{1,0:T(8,128)S(1)} %reduce.40) | data formatting | bytes 1572864
  1145.0 26.8 %copy.317 = f32[1,2,3,2,32,512]{5,4,3,2,1,0:T(8,128)S(1)} copy(f32[1,2,3,2,32,512]{2,3,1,5,4,0:T(2,128)} %bitcast.716) | data formatting | bytes 1572864 | tf_op jit(solution)/shard_map/all_to_all | solution.py:136
  1192.2 7.4 all-to-all-start.2
  1203.3 10.5 all-to-all-done.2
  (514 shorter events, 207.1 us)
Async XLA Ops:
  1.6 84.7 %copy-start = (f32[1,2,128,128]{3,2,1,0:T(8,128)S(1)}, f32[1,2,128,128]{3,2,1,0:T(8,128)}, u32[]{:S(2)}) copy-start(f32[1,2,128,128]{3,2,1,0:T(8,128)} %param.7) | copy-start | bytes 393220
  1.6 84.9 %copy-start.5 = (f32[1,2,128,128]{3,2,1,0:T(8,128)S(1)}, f32[1,2,128,128]{3,2,1,0:T(8,128)}, u32[]{:S(2)}) copy-start(f32[1,2,128,128]{3,2,1,0:T(8,128)} %param.6) | copy-start | bytes 393220
  1.7 85.1 %copy-start.6 = (f32[1,1,2,128,128]{4,3,2,1,0:T(8,128)S(1)}, f32[1,1,2,128,128]{4,3,2,1,0:T(8,128)}, u32[]{:S(2)}) copy-start(f32[1,1,2,128,128]{4,3,2,1,0:T(8,128)} %param.8) | copy-start | bytes 393220
  1.7 85.6 %collective-permute-start.2 = (f32[2,128,128]{1,2,0:T(8,128)S(1)}, f32[2,128,128]{1,2,0:T(8,128)S(1)}, u32[]{:S(2)}, u32[]{:S(2)}) collective-permute-start(f32[2,128,128]{1,2,0:T(8,128)S(1)} %bitcast.744), channel_id=1, source_target_pairs={{1,0},{2,1},{3,2},{4,3},{5,4},{6,5},{7,6},{9,8},{10,9},{11,10},{12... | collective-permute-start | bytes 393224 | tf_op jit(solution)/shard_map/ppermute | solution.py:15
  77.7 981.6 %all-to-all-start.1 = ((f32[32,1,6144]{2,1,0:T(1,128)}), f32[32,1,6144]{2,1,0:T(1,128)}, u32[]{:S(2)}, u32[]{:S(2)}) async-start(f32[32,1,6144]{2,1,0:T(1,128)} %reshape.1293), calls=%async_computation.1 | async-start | bytes 1572864 | tf_op jit(solution)/shard_map/all_to_all | solution.py:136
  205.7 6.8 collective-permute-start.1
  210.0 6.7 collective-permute-start
  334.8 5.5 collective-permute-start.1
  338.3 7.2 collective-permute-start
  463.6 6.2 collective-permute-start.1
  467.9 5.7 collective-permute-start
  591.6 5.5 collective-permute-start.1
  595.2 5.8 collective-permute-start
  719.0 5.6 collective-permute-start.1
  722.7 5.7 collective-permute-start
  846.4 4.7 collective-permute-start.1
  849.2 5.7 collective-permute-start
  972.9 5.1 collective-permute-start.1
  976.1 5.7 collective-permute-start
  1051.2 4.4 copy-start.3
  1052.6 3.0 copy-start.1
  1052.9 2.7 copy-start.2
  1054.7 1.0 copy-start.4
  1059.3 117.4 %all-to-all-start = ((f32[32,1,2,3,2,512]{5,4,3,2,1,0:T(2,128)}), f32[32,1,2,3,2,512]{5,4,3,2,1,0:T(2,128)S(1)}, u32[]{:S(2)}, u32[]{:S(2)}) async-start(f32[32,1,2,3,2,512]{5,4,3,2,1,0:T(2,128)} %copy.288), calls=%async_computation | async-start | bytes 1572864 | tf_op jit(solution)/shard_map/all_to_all | solution.py:131
  1192.2 21.6 %all-to-all-start.2 = ((f32[32,2,3,2,512]{4,3,2,1,0:T(2,128)}), f32[32,2,3,2,512]{4,3,2,1,0:T(2,128)S(1)}, u32[]{:S(2)}, u32[]{:S(2)}) async-start(f32[32,2,3,2,512]{4,3,2,1,0:T(2,128)} %copy.293), calls=%async_computation.2 | async-start | bytes 1572864 | tf_op jit(solution)/shard_map/all_to_all | solution.py:158
